TPU v7x, 512 devices: a whole 4x8x8 slice. The times are simulated.
512 devices in a mesh: depth: 16 (over x, z_hi), plane: 32 (over z_lo, y, core).
Axes of the slice: x: 4, y: 8, z: 8 (z_hi: 4, z_lo: 2; z = z_hi * 2 + z_lo), core: 2. Of those that a mesh axis runs over, the one named last changes fastest.
Arguments:
- volume: bfloat16 [64, 128, 128], P('depth', 'plane'), may hold values from -6 to 6
- cotangent: float32 [64, 128, 128], P('depth', 'plane'), may hold values from -6 to 6
- kernel_in: bfloat16 [27, 32], replicated, may hold values from -1.25 to 1.25
- kernel_mid: bfloat16 [27, 32, 32], replicated, may hold values from -0.21875 to 0.21875
- kernel_out: bfloat16 [27, 32], replicated, may hold values from -0.21875 to 0.21875
- measured: float32 [64, 32, 1024], P('depth'), may hold values from -24 to 24
- angle_ids: int32 [8], replicated, may hold values from 0 to 31, as said below
- ray_bins: int32 [8, 128, 128], P(None, 'plane'), may hold values from 0 to 1023, as said below
Outputs:
- grad_volume: float32 [64, 128, 128], P('depth', 'plane')
- grad_kernel_in: float32 [27, 32], replicated
- grad_kernel_mid: float32 [27, 32, 32], replicated
- grad_kernel_out: float32 [27, 32], replicated
Inputs may be any that keep to these rules, and one draw needn't show every extreme that they name: `angle_ids`: each entry names a measured view; the entries are distinct. `ray_bins`: for each view a, the bins follow parallel-beam geometry: a cell's bin is the detector position of its centre projected along the direction of view angle_ids[a], clipped at the detector's ends.
All inputs are finite; a program needn't handle non-finite values.
Results may differ from a plain program's by a relative error of at most 0.0051.
Values may be sent and summed in bfloat16 or wider, within the bound.
No kernel may reach another device: no remote copies, remote signals or barrier semaphores. Data moves between devices by JAX's collectives and lax.ppermute only.
A program may use at most 64 MiB of HBM per device.

v0:
```python
import jax
import jax.numpy as jnp
from jax import lax
from jax.sharding import PartitionSpec as P

BINS = 1024
ANG = 8
delta_scale = 6.0


def extended(cells, sides, width):
    for axis, dim in sides:
        count = lax.axis_size(axis)
        ends = count - 1
        head = lax.slice_in_dim(cells, 0, width, axis=dim)
        tail = lax.slice_in_dim(cells, cells.shape[dim] - width, cells.shape[dim], axis=dim)
        cells = jnp.concatenate(
            [
                lax.ppermute(tail, axis, [(i, (i + 1) % count) for i in range(ends)]),
                cells,
                lax.ppermute(head, axis, [((i + 1) % count, i) for i in range(ends)]),
            ],
            axis=dim,
        )
    return cells


def shifts():
    return [
        (step_z, step_y, step_x)
        for step_z in (-1, 0, 1)
        for step_y in (-1, 0, 1)
        for step_x in (-1, 0, 1)
    ]


def pad_row(field):
    return jnp.pad(field, ((0, 0), (0, 0), (0, 0), (1, 1)))


def extend(field):
    padded = extended(field, (("depth", 1), ("plane", 2)), 1)
    return pad_row(padded)


def window_at(padded, start_z, start_y, start_x, extent):
    return lax.slice(
        padded,
        (0, start_z, start_y, start_x),
        (padded.shape[0], start_z + extent[0], start_y + extent[1], start_x + extent[2]),
    )


def forward_conv(padded, kernel, extent, base):
    summed = jnp.zeros((kernel.shape[1],) + tuple(extent), jnp.float32)
    for position, (step_z, step_y, step_x) in enumerate(shifts()):
        window = window_at(padded, base[0] + step_z, base[1] + step_y, base[2] + step_x, extent)
        summed = summed + jnp.einsum(
            "oc,czhw->ozhw", kernel[position], window, preferred_element_type=jnp.float32
        )
    return summed


def adjoint_conv(padded, kernel, extent, base):
    summed = jnp.zeros((kernel.shape[2],) + tuple(extent), jnp.float32)
    for position, (step_z, step_y, step_x) in enumerate(shifts()):
        window = window_at(padded, base[0] - step_z, base[1] - step_y, base[2] - step_x, extent)
        summed = summed + jnp.einsum(
            "oc,ozhw->czhw", kernel[position], window, preferred_element_type=jnp.float32
        )
    return summed


def kernel_grad(grad_out, padded_in, extent, base):
    pieces = []
    for position, (step_z, step_y, step_x) in enumerate(shifts()):
        window = window_at(padded_in, base[0] + step_z, base[1] + step_y, base[2] + step_x, extent)
        pieces.append(
            jnp.einsum("ozhw,czhw->oc", grad_out, window, preferred_element_type=jnp.float32)
        )
    return jnp.stack(pieces)


def silu_slope(value):
    sigma = jax.nn.sigmoid(value)
    return sigma * (1.0 + value * (1.0 - sigma))


def project_pair(first, second, ray_bins):
    slices = first.shape[0]
    flattened = jnp.concatenate((first.reshape(slices, -1), second.reshape(slices, -1)), axis=0).T

    def one_view(bins_view):
        return jax.ops.segment_sum(flattened, bins_view.reshape(-1), num_segments=BINS)

    per_view = lax.map(one_view, ray_bins)
    stacked = jnp.transpose(per_view, (2, 0, 1))
    return (stacked[:slices], stacked[slices:])


def back_project(rays, ray_bins):

    def accumulate(summed, view_pair):
        rays_view, bins_view = view_pair
        return (summed + jnp.take(rays_view, bins_view.reshape(-1), axis=1), None)

    initial = jnp.zeros((rays.shape[0], ray_bins.shape[1] * ray_bins.shape[2]), rays.dtype)
    summed = lax.scan(accumulate, initial, (jnp.transpose(rays, (1, 0, 2)), ray_bins))[0]
    return summed.reshape(rays.shape[0], ray_bins.shape[1], ray_bins.shape[2])


def curvature(residual):
    ratio = residual / delta_scale
    inner = 1.0 + ratio * ratio
    return 1.0 / (inner * jnp.sqrt(inner))


def per_device(volume, cotangent, kernel_in, kernel_mid, kernel_out, measured, angle_ids, ray_bins):
    extent = volume.shape
    depth_rows, plane_rows, cells = extent
    first_in = kernel_in[:, :, None]
    last_out = kernel_out[:, None, :]
    source_pad = extend(volume[None])
    first_raw = forward_conv(source_pad, first_in, extent, (1, 1, 1))
    act_first = jax.nn.silu(first_raw).astype(jnp.bfloat16)
    slope_first = silu_slope(first_raw)
    first_pad = extend(act_first)
    second_raw = forward_conv(first_pad, kernel_mid, extent, (1, 1, 1))
    act_second = jax.nn.silu(second_raw).astype(jnp.bfloat16)
    slope_second = silu_slope(second_raw)
    second_pad = extend(act_second)
    residue = forward_conv(second_pad, last_out, extent, (1, 1, 1))[0]
    source_margin, first_margin, second_margin = (1, 1, 1)
    mid_margin, low_margin = (0, 0)
    denoised = volume.astype(jnp.float32) - residue
    chosen = jnp.take(measured, angle_ids, axis=1)
    local_rays, local_cot = project_pair(denoised, cotangent, ray_bins)
    forward_rays, cot_rays = lax.psum((local_rays, local_cot), "plane")
    weighted = curvature(forward_rays - chosen) * cot_rays
    grad_denoised = cotangent - 0.25 / ANG * back_project(weighted, ray_bins)
    cell_count = depth_rows * lax.axis_size("depth") * plane_rows * lax.axis_size("plane") * cells
    grad_scale = float(cell_count) ** (-0.5)
    grad_last = (-grad_denoised).astype(jnp.bfloat16)
    last_pad = extend(grad_last[None])
    mid_extent = (depth_rows + 2 * mid_margin, plane_rows + 2 * mid_margin, cells)
    low_extent = (depth_rows + 2 * low_margin, plane_rows + 2 * low_margin, cells)
    term_out = kernel_grad(grad_last[None], second_pad, extent, (second_margin, second_margin, 1))[
        :, 0, :
    ]
    grad_second = adjoint_conv(last_pad, last_out, mid_extent, (1, 1, 1))
    grad_mid = (grad_second * slope_second).astype(jnp.bfloat16)
    term_mid = kernel_grad(grad_mid, first_pad, extent, (first_margin, first_margin, 1))
    mid_pad = extend(grad_mid)
    grad_first = adjoint_conv(mid_pad, kernel_mid, low_extent, (1, 1, 1))
    grad_low = (grad_first * slope_first).astype(jnp.bfloat16)
    term_in = kernel_grad(grad_low, source_pad, extent, (source_margin, source_margin, 1))[:, :, 0]
    term_in, term_mid, term_out = lax.psum((term_in, term_mid, term_out), ("depth", "plane"))
    low_pad = extend(grad_low)
    grad_volume = grad_denoised + adjoint_conv(low_pad, first_in, extent, (1, 1, 1))[0]
    return (grad_volume, term_in * grad_scale, term_mid * grad_scale, term_out * grad_scale)


def solution(mesh):
    placed = (
        P("depth", "plane", None),
        P("depth", "plane", None),
        P(),
        P(),
        P(),
        P("depth", None, None),
        P(),
        P(None, "plane", None),
    )
    return jax.shard_map(
        per_device,
        mesh=mesh,
        in_specs=placed,
        out_specs=(P("depth", "plane", None), P(), P(), P()),
        check_vma=False,
    )
```

profile of v0, /device:TPU:64, one launch (start us, length us, event | category | flops | bytes accessed | tf_op | source)
XLA Modules:
  0.0 829.1 jit_solution(6284097332181020481)
XLA Ops:
  8.0 6.1 collective-permute-start
  23.7 1.9 collective-permute-start.2
  25.7 5.8 collective-permute-start.3
  36.5 7.0 collective-permute-start.4
  45.6 5.9 collective-permute-done.5
  51.5 1.9 collective-permute-start.6
  53.5 5.9 collective-permute-start.7
  70.3 5.9 collective-permute-start.8
  77.9 5.1 collective-permute-done.9
  84.9 5.8 collective-permute-start.11
  99.5 32.3 %while.21 = (s32[]{:T(128)}, f32[8,1024,8]{1,0,2:T(8,128)S(1)}, s32[8,4,128]{2,1,0:T(4,128)}, f32[512,8]{1,0:T(8,128)}, s32[]{:T(128)}, /*index=5*/f32[]{:T(128)}, s32[]{:T(128)}) while((s32[]{:T(128)}, f32[8,1024,8]{1,0,2:T(8,128)S(1)}, s32[8,4,128]{2,1,0:T(4,128)}, f32[512,8]{1,0:T(8,128)}, s32[]{:T(128)}, /*index=5*/f32[]{:T(128)}, ...), condition=%wide.region_2.3_spmd, body=%wide.region_0.2_spmd.sunk | while | flops 4098 | bytes 168533 | solution.py:96
  100.2 2.8 scatter_custom_fusion.5
  104.0 2.8 scatter_custom_fusion.5
  107.8 2.8 scatter_custom_fusion.5
  111.6 4.6 scatter_custom_fusion.5
  117.3 2.8 scatter_custom_fusion.5
  121.1 2.8 scatter_custom_fusion.5
  124.9 2.8 scatter_custom_fusion.5
  128.7 2.8 scatter_custom_fusion.5
  134.1 226.0 %all-reduce.13.cloned.1.call-done = (f32[4,8,1024]{2,1,0:T(8,128)}, f32[4,8,1024]{2,1,0:T(8,128)}) async-done(((f32[4,8,1024]{2,1,0:T(8,128)}, f32[4,8,1024]{2,1,0:T(8,128)}), (f32[4,8,1024]{2,1,0:T(8,128)}, f32[4,8,1024]{2,1,0:T(8,128)})) %all-reduce.13.cloned.1.call-update) | async-done | bytes 262160 | tf_op jit(solution)/shard_map/psum | solution.py:138
  361.2 17.5 %while.22 = (s32[]{:T(128)}, f32[4,512]{0,1:T(8,128)S(1)}, s32[8,4,128]{2,1,0:T(4,128)}, f32[8,4,1024]{2,0,1:T(8,128)S(1)}, s32[]{:T(128)}, /*index=5*/s32[]{:T(128)}) while((s32[]{:T(128)}, f32[4,512]{0,1:T(8,128)S(1)}, s32[8,4,128]{2,1,0:T(4,128)}, f32[8,4,1024]{2,0,1:T(8,128)S(1)}, s32[]{:T(128)}, /*index=5*/s32[]{:T(128)}) %tuple.247), condition=%wide.region_6.7_spmd.clone, body=%wide.region_5.6_spmd.clone.sunk | while | flops 11779 | bytes 123991 | solution.py:108
  379.0 4.8 collective-permute-start.12
  392.2 5.8 collective-permute-start.15
  406.9 6.2 collective-permute-start.16
  415.9 4.3 collective-permute-done.17
  420.2 4.6 collective-permute-start.19
  426.9 260.4 %all-reduce.11.cloned.1.call-done = f32[27,32,32]{2,1,0:T(8,128)} async-done(((f32[27,32,32]{2,1,0:T(8,128)}), f32[27,32,32]{2,1,0:T(8,128)}) %all-reduce.11.cloned.1.call-update) | async-done | bytes 110608 | tf_op jit(solution)/shard_map/psum | solution.py:157
  700.6 95.3 %all-reduce.6 = (f32[27,32]{1,0:T(8,128)S(1)}, f32[27,32]{1,0:T(8,128)S(1)}) all-reduce(f32[27,32]{1,0:T(8,128)S(1)} %bitcast.2037, f32[27,32]{1,0:T(8,128)S(1)} %bitcast.2036), channel_id=1, replica_groups=mesh['depth'=16,'plane'=32] {'depth','plane'}, use_global_device_ids=true, to_apply=%region_7.8 | all-reduce | flops 1728 | bytes 13824 | tf_op jit(solution)/shard_map/psum | solution.py:157
  796.5 4.6 collective-permute-start.20
  803.0 4.8 collective-permute-done.21
  809.8 2.4 collective-permute-start.22
  812.4 4.8 collective-permute-done.22
  (566 shorter events, 113.4 us)
Async XLA Ops:
  7.2 37.7 %copy-start = (f32[4,32,1024]{2,1,0:T(8,128)S(1)}, f32[4,32,1024]{2,1,0:T(8,128)}, u32[]{:S(2)}) copy-start(f32[4,32,1024]{2,1,0:T(8,128)} %param.17) | copy-start | bytes 1572868
  7.2 352.9 %all-reduce.13.cloned.1.call-start = ((), (), s32[]{:S(2)}) async-start(), calls=%async_computation.1 | async-start | bytes 524288 | tf_op jit(solution)/shard_map/psum | solution.py:138
  8.0 15.0 %collective-permute-start = (bf16[1,1,4,128]{3,2,1,0:T(4,128)(2,1)S(1)}, bf16[1,1,4,128]{3,2,1,0:T(4,128)(2,1)S(1)}, u32[]{:S(2)}, u32[]{:S(2)}) collective-permute-start(bf16[1,1,4,128]{3,2,1,0:T(4,128)(2,1)S(1)} %get-tuple-element.323), channel_id=1, source_target_pairs={{0,32},{32,64},{64,96},{96,128},{128,160},{160,192},{192,224},{224... | collective-permute-start | bytes 3080 | tf_op jit(solution)/shard_map/ppermute | solution.py:19
  14.1 9.0 %collective-permute-start.1 = (bf16[1,1,4,128]{3,2,1,0:T(4,128)(2,1)S(1)}, bf16[1,1,4,128]{3,2,1,0:T(4,128)(2,1)S(1)}, u32[]{:S(2)}, u32[]{:S(2)}) collective-permute-start(bf16[1,1,4,128]{3,2,1,0:T(4,128)(2,1)S(1)} %get-tuple-element.324), channel_id=1, source_target_pairs={{32,0},{64,32},{96,64},{128,96},{160,128},{192,160},{224,192},{256... | collective-permute-start | bytes 3080 | tf_op jit(solution)/shard_map/ppermute | solution.py:21
  23.7 9.1 %collective-permute-start.2 = (bf16[1,6,1,128]{3,2,1,0:T(2,128)(2,1)S(1)}, bf16[1,6,1,128]{3,2,1,0:T(2,128)(2,1)S(1)}, u32[]{:S(2)}, u32[]{:S(2)}) collective-permute-start(bf16[1,6,1,128]{3,2,1,0:T(2,128)(2,1)S(1)} %get-tuple-element.311), channel_id=1, source_target_pairs={{0,1},{1,2},{2,3},{3,4},{4,5},{5,6},{6,7},{7,8},{8,9},{9,10},{10,1... | collective-permute-start | bytes 4616 | tf_op jit(solution)/shard_map/ppermute | solution.py:19
  25.7 7.1 collective-permute-start.3
  36.5 9.2 %collective-permute-start.4 = (bf16[32,1,4,128]{3,0,2,1:T(8,128)(2,1)S(1)}, bf16[32,1,4,128]{3,0,2,1:T(8,128)(2,1)S(1)}, u32[]{:S(2)}, u32[]{:S(2)}) collective-permute-start(bf16[32,1,4,128]{3,0,2,1:T(8,128)(2,1)S(1)} %get-tuple-element.175), channel_id=1, source_target_pairs={{0,32},{32,64},{64,96},{96,128},{128,160},{160,192},{192,224},{224... | collective-permute-start | bytes 98312 | tf_op jit(solution)/shard_map/ppermute | solution.py:19
  43.5 8.0 collective-permute-start.5
  51.5 7.9 collective-permute-start.6
  53.5 7.6 collective-permute-start.7
  70.3 7.5 collective-permute-start.8
  76.3 6.7 collective-permute-start.9
  83.0 8.7 %collective-permute-start.10 = (bf16[32,6,1,128]{3,0,2,1:T(8,128)(2,1)S(1)}, bf16[32,6,1,128]{3,0,2,1:T(8,128)(2,1)S(1)}, u32[]{:S(2)}, u32[]{:S(2)}) collective-permute-start(bf16[32,6,1,128]{3,0,2,1:T(8,128)(2,1)S(1)} %get-tuple-element.159), channel_id=1, source_target_pairs={{0,1},{1,2},{2,3},{3,4},{4,5},{5,6},{6,7},{7,8},{8,9},{9,10},{10,1... | collective-permute-start | bytes 147464 | tf_op jit(solution)/shard_map/ppermute | solution.py:19
  84.9 7.5 collective-permute-start.11
  132.6 554.8 %all-reduce.11.cloned.1.call-start = ((), (), s32[]{:S(2)}) async-start(), calls=%async_computation | async-start | bytes 884736 | tf_op jit(solution)/shard_map/psum | solution.py:157
  133.4 226.8 %copy-start.96 = (pred[8]{0:T(512)(128)(4,1)S(1)}, pred[8]{0:T(512)(128)(4,1)}, u32[]{:S(2)}) copy-start(pred[8]{0:T(512)(128)(4,1)} %compare_and_fusion.1) | copy-start | bytes 28
  379.0 10.9 %collective-permute-start.12 = (bf16[1,1,4,128]{3,2,1,0:T(4,128)(2,1)S(1)}, bf16[1,1,4,128]{3,2,1,0:T(4,128)(2,1)S(1)}, u32[]{:S(2)}, u32[]{:S(2)}) collective-permute-start(bf16[1,1,4,128]{3,2,1,0:T(4,128)(2,1)S(1)} %get-tuple-element.321), channel_id=1, source_target_pairs={{0,32},{32,64},{64,96},{96,128},{128,160},{160,192},{192,224},{224... | collective-permute-start | bytes 3080 | tf_op jit(solution)/shard_map/ppermute | solution.py:19
  383.8 6.5 collective-permute-start.13
  388.9 10.7 %copy-start.71 = (f32[32]{0:T(128)S(1)}, f32[32]{0:T(128)}, u32[]{:S(2)}) copy-start(f32[32]{0:T(128)} %get-tuple-element.251) | copy-start | bytes 388
  388.9 10.7 %copy-start.72 = (f32[32]{0:T(128)S(1)}, f32[32]{0:T(128)}, u32[]{:S(2)}) copy-start(f32[32]{0:T(128)} %get-tuple-element.252) | copy-start | bytes 388
  388.9 10.7 %copy-start.73 = (f32[32]{0:T(128)S(1)}, f32[32]{0:T(128)}, u32[]{:S(2)}) copy-start(f32[32]{0:T(128)} %get-tuple-element.253) | copy-start | bytes 388
  388.9 10.7 %copy-start.74 = (f32[32]{0:T(128)S(1)}, f32[32]{0:T(128)}, u32[]{:S(2)}) copy-start(f32[32]{0:T(128)} %get-tuple-element.254) | copy-start | bytes 388
  390.3 7.7 collective-permute-start.14
  392.2 7.1 collective-permute-start.15
  406.9 9.0 %collective-permute-start.16 = (bf16[32,1,4,128]{3,0,2,1:T(8,128)(2,1)S(1)}, bf16[32,1,4,128]{3,0,2,1:T(8,128)(2,1)S(1)}, u32[]{:S(2)}, u32[]{:S(2)}) collective-permute-start(bf16[32,1,4,128]{3,0,2,1:T(8,128)(2,1)S(1)} %get-tuple-element.169), channel_id=1, source_target_pairs={{0,32},{32,64},{64,96},{96,128},{128,160},{160,192},{192,224},{224... | collective-permute-start | bytes 98312 | tf_op jit(solution)/shard_map/ppermute | solution.py:19
  413.1 7.1 collective-permute-start.17
  420.2 269.0 %collective-permute-start.19 = (bf16[32,6,1,128]{3,0,2,1:T(8,128)(2,1)S(1)}, bf16[32,6,1,128]{3,0,2,1:T(8,128)(2,1)S(1)}, u32[]{:S(2)}, u32[]{:S(2)}) collective-permute-start(bf16[32,6,1,128]{3,0,2,1:T(8,128)(2,1)S(1)} %get-tuple-element.156), channel_id=1, source_target_pairs={{1,0},{2,1},{3,2},{4,3},{5,4},{6,5},{7,6},{8,7},{9,8},{10,9},{11,1... | collective-permute-start | bytes 147464 | tf_op jit(solution)/shard_map/ppermute | solution.py:21
  424.8 264.4 %collective-permute-start.18 = (bf16[32,6,1,128]{3,0,2,1:T(8,128)(2,1)S(1)}, bf16[32,6,1,128]{3,0,2,1:T(8,128)(2,1)S(1)}, u32[]{:S(2)}, u32[]{:S(2)}) collective-permute-start(bf16[32,6,1,128]{3,0,2,1:T(8,128)(2,1)S(1)} %get-tuple-element.155), channel_id=1, source_target_pairs={{0,1},{1,2},{2,3},{3,4},{4,5},{5,6},{6,7},{7,8},{8,9},{9,10},{10,1... | collective-permute-start | bytes 147464 | tf_op jit(solution)/shard_map/ppermute | solution.py:19
  796.5 6.5 collective-permute-start.20
  801.1 6.7 collective-permute-start.21
  807.8 4.6 collective-permute-start.23
  809.8 7.5 collective-permute-start.22
  (91 other events, 401.5 us)
Sparse Core Ops, SparseCore 0:
  132.7 227.3 all-reduce.12
  416.0 271.3 all-reduce.10
where the time goes:
time: 831 us; the launch traced here: 829 us
  waiting for transfers between devices  516 us (62%)
  blocking collectives  95.3 us (11%)
  starting transfers between devices  84.2 us (10%)
  other arithmetic  52.3 us (6%)
  matrix products  32.7 us (4%)
  local copies, waits for them, and re-layouts  32.5 us (4%)
  between operations  15.8 us (2%)
    psum x1, waiting for transfers between devices, per_device(): lax.psum((term_in, term_mid, term_out), ('depth', 'plane'))  260 us
    psum x1, waiting for transfers between devices, per_device(): forward_rays, cot_rays = lax.psum((local_rays, local_cot), 'plane')  226 us
    psum x1, blocking collectives, per_device(): lax.psum((term_in, term_mid, term_out), ('depth', 'plane'))  95.3 us
    ppermute x12, starting transfers between devices, extended(): lax.ppermute(tail, axis, [(i, (i + 1) % count) for i in range(ends)])  46.5 us
    ppermute x12, starting transfers between devices, extended(): lax.ppermute(head, axis, [((i + 1) % count, i) for i in range(ends)])  37.6 us
    ppermute x12, waiting for transfers between devices, extended(): lax.ppermute(head, axis, [((i + 1) % count, i) for i in range(ends)])  24.2 us
    scatter-add x8, other arithmetic, one_view(): jax.ops.segment_sum(flattened, bins_view.reshape(-1), num_segments=BINS)  24 us
  transfers between devices with their start and end apart: 26, of which 12 were waited for; matrix products, arithmetic and copies ran while one was open for 2% of the time, Pallas kernels for 0%

commit v1 on v0

--- a/solution.py
+++ b/solution.py
@@ -154,7 +154,9 @@
     grad_first = adjoint_conv(mid_pad, kernel_mid, low_extent, (1, 1, 1))
     grad_low = (grad_first * slope_first).astype(jnp.bfloat16)
     term_in = kernel_grad(grad_low, source_pad, extent, (source_margin, source_margin, 1))[:, :, 0]
-    term_in, term_mid, term_out = lax.psum((term_in, term_mid, term_out), ("depth", "plane"))
+    term_in, term_mid, term_out = lax.psum(
+        lax.psum((term_in, term_mid, term_out), "depth"), "plane"
+    )
     low_pad = extend(grad_low)
     grad_volume = grad_denoised + adjoint_conv(low_pad, first_in, extent, (1, 1, 1))[0]
     return (grad_volume, term_in * grad_scale, term_mid * grad_scale, term_out * grad_scale)

time: 831 us -> 865 us (1.041)
  the two profiles are of different devices: /device:TPU:64 before, /device:TPU:1 now
where the time goes in v1:
time: 865 us; the launch traced here: 863 us
  waiting for transfers between devices  464 us (54%)
  blocking collectives  185 us (21%)
  starting transfers between devices  74.8 us (9%)
  other arithmetic  55.7 us (6%)
  matrix products  34.3 us (4%)
  local copies, waits for them, and re-layouts  32.4 us (4%)
  between operations  15.5 us (2%)
    psum x1, waiting for transfers between devices, per_device(): forward_rays, cot_rays = lax.psum((local_rays, local_cot), 'plane')  227 us
    psum x1, waiting for transfers between devices, per_device(): lax.psum(lax.psum((term_in, term_mid, term_out), 'depth'), 'plane')  209 us
    psum x1, blocking collectives, per_device(): lax.psum(lax.psum((term_in, term_mid, term_out), 'depth'), 'plane')  117 us
    psum x1, blocking collectives, per_device(): lax.psum((term_in, term_mid, term_out), 'depth')  68.5 us
    ppermute x12, starting transfers between devices, extended(): lax.ppermute(tail, axis, [(i, (i + 1) % count) for i in range(ends)])  49 us
    scatter-add x8, other arithmetic, one_view(): jax.ops.segment_sum(flattened, bins_view.reshape(-1), num_segments=BINS)  27.5 us
    ppermute x12, waiting for transfers between devices, extended(): lax.ppermute(head, axis, [((i + 1) % count, i) for i in range(ends)])  26.6 us
    ppermute x12, starting transfers between devices, extended(): lax.ppermute(head, axis, [((i + 1) % count, i) for i in range(ends)])  25.7 us
  transfers between devices with their start and end apart: 27, of which 12 were waited for; matrix products, arithmetic and copies ran while one was open for 4% of the time, Pallas kernels for 0%

profile of v1, /device:TPU:1, one launch (start us, length us, event | category | flops | bytes accessed | tf_op | source)
XLA Modules:
  0.0 863.1 jit_solution(5156873765815244062)
XLA Ops:
  8.0 6.6 collective-permute-start
  24.3 4.0 collective-permute-start.2
  37.0 7.6 collective-permute-start.4
  46.7 4.9 collective-permute-done.5
  51.7 3.2 collective-permute-start.6
  57.0 3.4 collective-permute-done.7
  69.6 5.8 collective-permute-start.8
  76.8 4.1 collective-permute-done.9
  81.0 3.3 collective-permute-start.10
  87.2 2.5 collective-permute-done.11
  96.8 35.7 %while.21 = (s32[]{:T(128)}, f32[8,1024,8]{1,0,2:T(8,128)S(1)}, s32[8,4,128]{2,1,0:T(4,128)}, f32[512,8]{1,0:T(8,128)}, s32[]{:T(128)}, /*index=5*/f32[]{:T(128)}, s32[]{:T(128)}) while((s32[]{:T(128)}, f32[8,1024,8]{1,0,2:T(8,128)S(1)}, s32[8,4,128]{2,1,0:T(4,128)}, f32[512,8]{1,0:T(8,128)}, s32[]{:T(128)}, /*index=5*/f32[]{:T(128)}, ...), condition=%wide.region_2.3_spmd, body=%wide.region_0.2_spmd.sunk | while | flops 4098 | bytes 168533 | solution.py:96
  97.5 3.5 scatter_custom_fusion.5
  102.0 3.2 scatter_custom_fusion.5
  106.2 3.2 scatter_custom_fusion.5
  110.5 4.6 scatter_custom_fusion.5
  116.1 3.0 scatter_custom_fusion.5
  120.2 3.3 scatter_custom_fusion.5
  124.5 3.5 scatter_custom_fusion.5
  129.0 3.2 scatter_custom_fusion.5
  134.8 227.3 %all-reduce.17.cloned.1.call-done = (f32[4,8,1024]{2,1,0:T(8,128)}, f32[4,8,1024]{2,1,0:T(8,128)}) async-done(((f32[4,8,1024]{2,1,0:T(8,128)}, f32[4,8,1024]{2,1,0:T(8,128)}), (f32[4,8,1024]{2,1,0:T(8,128)}, f32[4,8,1024]{2,1,0:T(8,128)})) %all-reduce.17.cloned.1.call-update) | async-done | bytes 262160 | tf_op jit(solution)/shard_map/psum | solution.py:138
  363.2 17.5 %while.22 = (s32[]{:T(128)}, f32[4,512]{0,1:T(8,128)S(1)}, s32[8,4,128]{2,1,0:T(4,128)}, f32[8,4,1024]{2,0,1:T(8,128)S(1)}, s32[]{:T(128)}, /*index=5*/s32[]{:T(128)}) while((s32[]{:T(128)}, f32[4,512]{0,1:T(8,128)S(1)}, s32[8,4,128]{2,1,0:T(4,128)}, f32[8,4,1024]{2,0,1:T(8,128)S(1)}, s32[]{:T(128)}, /*index=5*/s32[]{:T(128)}) %tuple.249), condition=%wide.region_6.7_spmd.clone, body=%wide.region_5.6_spmd.clone.sunk | while | flops 11779 | bytes 123991 | solution.py:108
  381.0 4.5 collective-permute-start.12
  395.2 2.4 collective-permute-start.15
  397.6 2.5 collective-permute-done.15
  407.7 5.4 collective-permute-start.16
  416.0 3.9 collective-permute-done.17
  422.2 3.4 collective-permute-start.18
  438.1 68.5 %all-reduce.8 = (f32[27,32]{1,0:T(8,128)S(1)}, f32[27,32]{1,0:T(8,128)S(1)}) all-reduce(f32[27,32]{1,0:T(8,128)S(1)} %bitcast.2037, f32[27,32]{1,0:T(8,128)S(1)} %bitcast.2036), channel_id=1, replica_groups=mesh['depth'=16,'plane'=32] {'depth'}, use_global_device_ids=true, to_apply=%region_7.8 | all-reduce | flops 1728 | bytes 13824 | tf_op jit(solution)/shard_map/psum | solution.py:158
  506.6 116.8 %all-reduce.6 = (f32[27,32]{1,0:T(8,128)S(1)}, f32[27,32]{1,0:T(8,128)S(1)}) all-reduce(f32[27,32]{1,0:T(8,128)S(1)} %get-tuple-element.97, f32[27,32]{1,0:T(8,128)S(1)} %get-tuple-element.98), channel_id=1, replica_groups=mesh['depth'=16,'plane'=32] {'plane'}, use_global_device_ids=true, to_apply=%region_8.9 | all-reduce | flops 1728 | bytes 13824 | tf_op jit(solution)/shard_map/psum | solution.py:157
  627.2 3.6 collective-permute-done.21
  630.8 7.3 collective-permute-start.23
  646.2 208.6 %all-reduce.15.cloned.1.call-done = f32[27,32,32]{2,1,0:T(8,128)} async-done(((f32[27,32,32]{2,1,0:T(8,128)}), f32[27,32,32]{2,1,0:T(8,128)}) %all-reduce.15.cloned.1.call-update) | async-done | bytes 110608 | tf_op jit(solution)/shard_map/psum | solution.py:157
  (576 shorter events, 119.8 us)
Async XLA Ops:
  7.2 38.8 %copy-start = (f32[4,32,1024]{2,1,0:T(8,128)S(1)}, f32[4,32,1024]{2,1,0:T(8,128)}, u32[]{:S(2)}) copy-start(f32[4,32,1024]{2,1,0:T(8,128)} %param.17) | copy-start | bytes 1572868
  7.2 354.9 %all-reduce.17.cloned.1.call-start = ((), (), s32[]{:S(2)}) async-start(), calls=%async_computation.2 | async-start | bytes 524288 | tf_op jit(solution)/shard_map/psum | solution.py:138
  8.0 15.6 %collective-permute-start = (bf16[1,1,4,128]{3,2,1,0:T(4,128)(2,1)S(1)}, bf16[1,1,4,128]{3,2,1,0:T(4,128)(2,1)S(1)}, u32[]{:S(2)}, u32[]{:S(2)}) collective-permute-start(bf16[1,1,4,128]{3,2,1,0:T(4,128)(2,1)S(1)} %get-tuple-element.325), channel_id=1, source_target_pairs={{0,32},{32,64},{64,96},{96,128},{128,160},{160,192},{192,224},{224... | collective-permute-start | bytes 3080 | tf_op jit(solution)/shard_map/ppermute | solution.py:19
  14.6 9.0 %collective-permute-start.1 = (bf16[1,1,4,128]{3,2,1,0:T(4,128)(2,1)S(1)}, bf16[1,1,4,128]{3,2,1,0:T(4,128)(2,1)S(1)}, u32[]{:S(2)}, u32[]{:S(2)}) collective-permute-start(bf16[1,1,4,128]{3,2,1,0:T(4,128)(2,1)S(1)} %get-tuple-element.326), channel_id=1, source_target_pairs={{32,0},{64,32},{96,64},{128,96},{160,128},{192,160},{224,192},{256... | collective-permute-start | bytes 3080 | tf_op jit(solution)/shard_map/ppermute | solution.py:21
  24.3 7.3 collective-permute-start.2
  28.4 4.9 collective-permute-start.3
  34.8 11.2 %copy-start.52 = (f32[4,4,128]{2,1,0:T(4,128)S(1)}, f32[4,4,128]{2,1,0:T(4,128)}, u32[]{:S(2)}) copy-start(f32[4,4,128]{2,1,0:T(4,128)} %param.13) | copy-start | bytes 24580
  37.0 9.8 %collective-permute-start.4 = (bf16[32,1,4,128]{3,0,2,1:T(8,128)(2,1)S(1)}, bf16[32,1,4,128]{3,0,2,1:T(8,128)(2,1)S(1)}, u32[]{:S(2)}, u32[]{:S(2)}) collective-permute-start(bf16[32,1,4,128]{3,0,2,1:T(8,128)(2,1)S(1)} %get-tuple-element.177), channel_id=1, source_target_pairs={{0,32},{32,64},{64,96},{96,128},{128,160},{160,192},{192,224},{224... | collective-permute-start | bytes 98312 | tf_op jit(solution)/shard_map/ppermute | solution.py:19
  44.6 7.1 collective-permute-start.5
  51.7 5.3 collective-permute-start.6
  54.9 5.5 collective-permute-start.7
  69.6 7.2 collective-permute-start.8
  75.4 5.6 collective-permute-start.9
  81.0 6.3 collective-permute-start.10
  84.3 5.4 collective-permute-start.11
  133.2 493.9 %all-reduce.13.cloned.1.call-start = ((), (), s32[]{:S(2)}) async-start(), calls=%async_computation | async-start | bytes 884736 | tf_op jit(solution)/shard_map/psum | solution.py:158
  134.0 228.1 %copy-start.96 = (pred[8]{0:T(512)(128)(4,1)S(1)}, pred[8]{0:T(512)(128)(4,1)}, u32[]{:S(2)}) copy-start(pred[8]{0:T(512)(128)(4,1)} %compare_and_fusion.1) | copy-start | bytes 28
  380.8 8.5 copy-start.38
  380.9 8.5 copy-start.37
  381.0 12.2 %collective-permute-start.12 = (bf16[1,1,4,128]{3,2,1,0:T(4,128)(2,1)S(1)}, bf16[1,1,4,128]{3,2,1,0:T(4,128)(2,1)S(1)}, u32[]{:S(2)}, u32[]{:S(2)}) collective-permute-start(bf16[1,1,4,128]{3,2,1,0:T(4,128)(2,1)S(1)} %get-tuple-element.323), channel_id=1, source_target_pairs={{0,32},{32,64},{64,96},{96,128},{128,160},{160,192},{192,224},{224... | collective-permute-start | bytes 3080 | tf_op jit(solution)/shard_map/ppermute | solution.py:19
  385.5 7.7 collective-permute-start.13
  393.2 4.4 collective-permute-start.14
  395.2 4.9 collective-permute-start.15
  407.7 8.3 collective-permute-start.16
  413.2 6.8 collective-permute-start.17
  416.0 438.8 %all-reduce.15.cloned.1.call-start = ((), (), s32[]{:S(2)}) async-start(), calls=%async_computation.1 | async-start | bytes 884736 | tf_op jit(solution)/shard_map/psum | solution.py:157
  420.0 5.8 collective-permute-start.19
  422.2 4.5 collective-permute-start.18
  624.0 3.2 collective-permute-start.20
  625.2 5.6 collective-permute-start.21
  630.8 9.5 %collective-permute-start.23 = (bf16[32,6,1,128]{3,0,2,1:T(8,128)(2,1)S(1)}, bf16[32,6,1,128]{3,0,2,1:T(8,128)(2,1)S(1)}, u32[]{:S(2)}, u32[]{:S(2)}) collective-permute-start(bf16[32,6,1,128]{3,0,2,1:T(8,128)(2,1)S(1)} %get-tuple-element.156), channel_id=1, source_target_pairs={{1,0},{2,1},{3,2},{4,3},{5,4},{6,5},{7,6},{8,7},{9,8},{10,9},{11,1... | collective-permute-start | bytes 147464 | tf_op jit(solution)/shard_map/ppermute | solution.py:21
  638.1 3.1 collective-permute-start.22
  (95 other events, 357.6 us)
Sparse Core Ops, SparseCore 0:
  133.4 228.6 all-reduce.16
  416.1 164.7 all-reduce.12
  627.3 227.4 all-reduce.14
